TPU v7x, 256 devices: a whole 4x4x8 slice. The times are simulated.
256 devices in a mesh: seq: 64 (over y, z, core), tp: 4 (over x).
Axes of the slice: x: 4, y: 4, z: 8, core: 2. Of those that a mesh axis runs over, the one named last changes fastest.
Arguments:
- stream: bfloat16 [8192, 2048], P('seq'), may hold values from -256 to 256
- lengths: int32 [6], replicated, may hold values from 1 to 7168, 8192 in all
- q_weight: bfloat16 [2048, 1536], P(None, 'tp'), may hold values from -0.125 to 0.125
- kv_down: bfloat16 [2048, 576], replicated, may hold values from -0.125 to 0.125
- latent_gain: float32 [512], replicated, may hold values from 0.1 to 1.9
- kv_up: bfloat16 [8, 512, 256], P('tp'), may hold values from -0.25 to 0.25
- out_weight: bfloat16 [1024, 2048], P('tp'), may hold values from -0.1875 to 0.1875
- moe_gain: float32 [2048], replicated, may hold values from 0.1 to 1.9
- routes: int32 [8192, 6], P('seq'), may hold values from 0 to 63, all different within a row; in each aligned block of 128 rows (0 to 127, 128 to 255, ...) at most 24 rows name the same one
- route_weight: float32 [8192, 6], P('seq'), may hold values from 0.05 to 0.5
- expert_gate: bfloat16 [64, 2048, 1408], P('seq', None, 'tp'), may hold values from -0.125 to 0.125
- expert_up: bfloat16 [64, 2048, 1408], P('seq', None, 'tp'), may hold values from -0.125 to 0.125
- expert_down: bfloat16 [64, 1408, 2048], P('seq', 'tp'), may hold values from -0.15625 to 0.15625
Outputs:
- layer_out: bfloat16 [8192, 2048], P('seq')
- latent_cache: bfloat16 [8192, 576], P('seq')
Inputs may be any that keep to these rules, and one draw needn't show every extreme that they name: 6 lengths summing to 8192, the longest exactly 7168. In each aligned block of 128 rows no expert is named by more than 24 routes, a bound that some block reaches.
All inputs are finite; a program needn't handle non-finite values.
Results may differ from a plain program's by a relative error of at most 0.0075.
Values may be sent and summed in bfloat16 or wider, within the bound.
A program may use at most 128 MiB of HBM per device.

v0:
```python
import jax
import jax.numpy as jnp
from jax import lax
from jax.sharding import PartitionSpec as P

D = 2048
NOPE = 128
ROPE = 64
LATENT = 512
VDIM = 128
THETA = 50000.0


def place(token_index, lengths):
    prompt_ends = jnp.cumsum(lengths)
    before = (prompt_ends[None, :] <= token_index[:, None]).astype(jnp.int32)
    segment = jnp.sum(before, axis=1)
    prompt_start = jnp.sum(before * lengths[None, :], axis=1)
    return (segment, token_index - prompt_start)


def angles(position):
    half_rope = ROPE // 2
    frequency = THETA ** (-2.0 * jnp.arange(half_rope, dtype=jnp.float32) / ROPE)
    angle_table = position.astype(jnp.float32)[:, None] * frequency[None, :]
    return (jnp.cos(angle_table), jnp.sin(angle_table))


def rotate(values, cos_table, sin_table):
    half_rope = ROPE // 2
    first_half = values[..., :half_rope]
    second = values[..., half_rope:]
    return jnp.concatenate(
        [first_half * cos_table - second * sin_table, first_half * sin_table + second * cos_table],
        axis=-1,
    )


def on_device(
    stream,
    lengths,
    q_weight,
    kv_down,
    latent_gain,
    kv_up,
    out_weight,
    moe_gain,
    routes,
    route_weight,
    expert_gate,
    expert_up,
    expert_down,
):
    tok_count = stream.shape[0]
    head_count = kv_up.shape[0]
    first_row = lax.axis_index("seq") * tok_count
    token_index = first_row + jnp.arange(tok_count, dtype=jnp.int32)
    segment, position = place(token_index, lengths)
    cos_table, sin_table = angles(position)
    kv_proj = jnp.dot(stream, kv_down, preferred_element_type=jnp.float32)
    compressed = kv_proj[:, :LATENT]
    factor = lax.rsqrt(jnp.mean(compressed * compressed, axis=1, keepdims=True) + 1e-06)
    latent = jnp.concatenate(
        [
            compressed * factor * latent_gain[None, :],
            rotate(kv_proj[:, LATENT:], cos_table, sin_table),
        ],
        axis=1,
    ).astype(jnp.bfloat16)
    q_proj = jnp.dot(stream, q_weight, preferred_element_type=jnp.float32).astype(jnp.bfloat16)
    q_proj = q_proj.reshape(tok_count, head_count, NOPE + ROPE)
    absorbed = jnp.einsum(
        "thj,hcj->thc", q_proj[:, :, :NOPE], kv_up[:, :, :NOPE], preferred_element_type=jnp.float32
    )
    rotated = rotate(
        q_proj[:, :, NOPE:].astype(jnp.float32), cos_table[:, None, :], sin_table[:, None, :]
    )
    softmax_scale = (NOPE + ROPE) ** (-0.5)
    queries = (jnp.concatenate([absorbed, rotated], axis=2) * softmax_scale).astype(jnp.bfloat16)
    queries = queries.reshape(tok_count * head_count, LATENT + ROPE)
    row_segment = jnp.repeat(segment, head_count)
    row_index = jnp.repeat(token_index, head_count)
    row_total = tok_count * head_count
    shard_rows = lax.all_gather(latent, "seq", axis=0, tiled=True)
    key_count = shard_rows.shape[0]
    key_index = jnp.arange(key_count, dtype=jnp.int32)
    key_segment, unused = place(key_index, lengths)
    allowed = (row_segment[:, None] == key_segment[None, :]) & (
        key_index[None, :] <= row_index[:, None]
    )
    running_max = jnp.full((row_total,), -1e30, jnp.float32)
    scores = jnp.einsum("ra,ka->rk", queries, shard_rows, preferred_element_type=jnp.float32)
    block_peak = jnp.max(jnp.where(allowed, scores, -jnp.inf), axis=1)
    new_peak = jnp.maximum(running_max, block_peak)
    weights = jnp.where(allowed, jnp.exp(scores - new_peak[:, None]), 0.0)
    running_sum = jnp.sum(weights, axis=1)
    context_sum = jnp.dot(
        weights.astype(jnp.bfloat16), shard_rows[:, :LATENT], preferred_element_type=jnp.float32
    )
    running_max, running_sum, context_sum = (new_peak, running_sum, context_sum)
    context = (context_sum / running_sum[:, None]).reshape(tok_count, head_count, LATENT)
    heads_out = jnp.einsum(
        "thc,hcv->thv",
        context,
        kv_up[:, :, NOPE:].astype(jnp.float32),
        precision=lax.Precision.HIGHEST,
    )
    heads_out = heads_out.astype(jnp.bfloat16).reshape(tok_count, head_count * VDIM)
    partial_attention = jnp.dot(heads_out, out_weight, preferred_element_type=jnp.float32)
    tp_count = lax.axis_size("tp")
    col_width = D // tp_count
    col_start = lax.axis_index("tp") * col_width
    attention_pieces = partial_attention.astype(jnp.bfloat16).reshape(
        tok_count, tp_count, col_width
    )
    attention_pieces = lax.all_to_all(
        attention_pieces.transpose(1, 0, 2), "tp", split_axis=0, concat_axis=0, tiled=True
    )
    attention_part = jnp.sum(attention_pieces.astype(jnp.float32), axis=0)
    stream_part = lax.dynamic_slice_in_dim(stream, col_start, col_width, 1)
    hidden = stream_part.astype(jnp.float32) + attention_part
    normed = hidden.astype(jnp.bfloat16)
    experts = lax.axis_size("seq")
    top_k = routes.shape[1]
    capacity = min(tok_count, max(2, 2 * tok_count * top_k // experts))
    flat_routes = routes.reshape(-1)
    onehot = (flat_routes[:, None] == jnp.arange(experts, dtype=jnp.int32)[None, :]).astype(
        jnp.int32
    )
    slot_rank = jnp.sum((jnp.cumsum(onehot, axis=0) - onehot) * onehot, axis=1)
    slot_index = flat_routes * capacity + slot_rank
    slot_table = (
        slot_index[:, None] == jnp.arange(experts * capacity, dtype=jnp.int32)[None, :]
    ).astype(jnp.bfloat16)
    placing = jnp.sum(slot_table.reshape(tok_count, top_k, experts * capacity), axis=1)
    outgoing = jnp.einsum("ts,td->sd", placing, normed, preferred_element_type=jnp.float32).astype(
        jnp.bfloat16
    )
    outgoing = outgoing.reshape(experts, capacity, col_width)
    chunk_count = 2
    chunk_slots = capacity // chunk_count
    returned_chunks = []
    for chunk in range(chunk_count):
        sending = outgoing[:, chunk * chunk_slots : (chunk + 1) * chunk_slots]
        received = lax.all_to_all(sending, "seq", split_axis=0, concat_axis=0, tiled=True)
        sources, slot_count, _ = received.shape
        flat_part = received.reshape(sources * slot_count, col_width)
        flat_rows = lax.all_gather(flat_part, "tp", axis=1, tiled=True).astype(jnp.float32)
        flat_rows = (
            flat_rows
            * lax.rsqrt(jnp.mean(flat_rows * flat_rows, axis=1, keepdims=True) + 1e-06)
            * moe_gain[None, :]
        ).astype(jnp.bfloat16)
        gate_act = jnp.dot(flat_rows, expert_gate[0], preferred_element_type=jnp.float32)
        up_act = jnp.dot(flat_rows, expert_up[0], preferred_element_type=jnp.float32)
        hidden_units = (jax.nn.silu(gate_act) * up_act).astype(jnp.bfloat16)
        expert_out = jnp.dot(
            hidden_units, expert_down[0], preferred_element_type=jnp.float32
        ).astype(jnp.bfloat16)
        expert_sum = lax.psum_scatter(expert_out, "tp", scatter_dimension=1, tiled=True)
        expert_sum = expert_sum.reshape(sources, slot_count, col_width)
        returned_chunks.append(
            lax.all_to_all(expert_sum, "seq", split_axis=0, concat_axis=0, tiled=True)
        )
    returned = jnp.concatenate(returned_chunks, axis=1)
    gathered = returned.reshape(experts * capacity, col_width)[slot_index].reshape(
        tok_count, top_k, col_width
    )
    moe = jnp.zeros((tok_count, col_width), jnp.float32)
    for route_slot in range(top_k):
        moe = moe + route_weight[:, route_slot][:, None] * gathered[:, route_slot].astype(
            jnp.float32
        )
    layer_part = (hidden + moe).astype(jnp.bfloat16)
    repeated_part = jnp.broadcast_to(layer_part[None], (tp_count,) + layer_part.shape)
    layer_pieces = lax.all_to_all(repeated_part, "tp", split_axis=0, concat_axis=0, tiled=True)
    layer_out = layer_pieces.transpose(1, 0, 2).reshape(tok_count, D)
    return (layer_out, latent)


def solution(mesh):
    return jax.shard_map(
        on_device,
        mesh=mesh,
        in_specs=(
            P("seq", None),
            P(),
            P(None, "tp"),
            P(),
            P(),
            P("tp", None, None),
            P("tp", None),
            P(),
            P("seq", None),
            P("seq", None),
            P("seq", None, "tp"),
            P("seq", None, "tp"),
            P("seq", "tp", None),
        ),
        out_specs=(P("seq", None), P("seq", None)),
        check_vma=False,
    )
```

profile of v0, /device:TPU:1, one launch (start us, length us, event | category | flops | bytes accessed | tf_op | source)
XLA Modules:
  0.0 411.8 jit_solution(14239379274214092569)
XLA Ops:
  7.3 1.0 reduce-window.18
  8.3 0.7 fusion.82
  9.1 1.9 fusion.94
  11.0 0.1 multiply_cosine_fusion
  11.2 0.1 multiply_convert_fusion
  11.3 0.7 pad_maximum_fusion.1
  12.2 0.1 eq.62
  12.3 0.1 eq.58
  12.4 1.8 convolution_convert_fusion.4
  14.3 0.1 copy.93
  14.4 0.1 copy.96
  14.6 0.1 copy.97
  14.8 0.2 eq.54
  15.0 0.2 le.48
  15.2 0.3 convolution_bitcast_fusion
  15.4 0.4 copy.95
  15.8 0.4 concatenate.17
  16.2 1.8 reduce-window.19
  18.0 0.3 slice_reduce_fusion
  18.3 0.1 fusion.76
  18.5 0.1 reduce_sum.104
  18.6 0.2 convert_reduce_fusion.1
  18.8 84.7 %all-gather.4.cloned.1.call-done = bf16[8192,576]{0,1:T(8,128)(2,1)} async-done(((bf16[128,576]{0,1:T(8,128)(2,1)}), bf16[8192,576]{0,1:T(8,128)(2,1)}) %all-gather.4.cloned.1.call-update) | async-done | bytes 9437200 | tf_op jit(solution)/shard_map/all_gather | solution.py:84
  103.5 6.8 %select_reduce_fusion = (f32[256]{0:T(256)S(1)}, f32[256,8192]{1,0:T(8,128)S(1)}) fusion(s32[256]{0:T(256)S(1)} %le.48, s32[8192]{0:T(1024)S(1)} %convert_reduce_fusion.1, s32[256]{0:T(256)S(1)} %eq.54, bf16[8192,576]{0,1:T(8,128)(2,1)} %all-gather.4.cloned.1.call-done, f32[256,32]{1,0:T(8,128)S(1)} %bitcast.130, f32[256,32]{1,0:T(8,128)S(1)} %bitcast.129, ...), kind=kOutput, calls=%fused_computation.4 | convolution fusion | flops 2426994432 | bytes 18451456 | tf_op jit(solution)/shard_map/ra,ka->rk/dot_general | solution.py:92
  110.3 2.8 fusion.9
  113.1 6.3 %fusion.41 = f32[256,512]{1,0:T(8,128)S(1)} fusion(bf16[8192,576]{0,1:T(8,128)(2,1)} %all-gather.4.cloned.1.call-done, f32[256,8192]{1,0:T(8,128)S(1)} %get-tuple-element.33, f32[256]{0:T(256)S(1)} %broadcast_maximum_fusion, s32[256]{0:T(256)S(1)} %le.48, s32[8192]{0:T(1024)S(1)} %convert_reduce_fusion.1, s32[256]{0:T(256)S(1)} %eq.54, f32[256]{0:T(256)S(1)} %fusion.9), kind=kOutput, calls=%fused_computation.49 | convolution fusion | flops 2160197632 | bytes 17338368 | tf_op jit(solution)/shard_map/dot_general | solution.py:97
  119.5 0.3 reshape.240
  119.8 0.5 convolution_convert_fusion.5
  120.3 0.3 convolution_convert_fusion.3
  120.6 0.8 copy.143
  121.5 4.0 all-to-all-start
  125.5 0.7 fusion.18
  126.2 8.2 %all-to-all-done = bf16[4,128,512]{2,1,0:T(8,128)(2,1)S(1)} async-done(((bf16[4,128,512]{2,1,0:T(8,128)(2,1)}), bf16[4,128,512]{2,1,0:T(8,128)(2,1)S(1)}, u32[]{:S(2)}, u32[]{:S(2)}) %all-to-all-start) | async-done | bytes 524320 | tf_op jit(solution)/shard_map/all_to_all | solution.py:116
  134.5 0.6 convolution_convert_fusion.2
  135.2 0.5 fusion.92
  135.7 39.2 %all_to_all.30 = bf16[64,12,512]{2,1,0:T(8,128)(2,1)S(1)} all-to-all(bf16[64,12,512]{2,1,0:T(8,128)(2,1)S(1)} %get-tuple-element.8), channel_id=1, replica_groups=mesh['seq'=64,'tp'=4] {'seq'}, dimensions={0} | all-to-all | bytes 1572864 | tf_op jit(solution)/shard_map/all_to_all | solution.py:145
  174.9 1.1 reshape.245
  176.0 34.5 %all_to_all.31 = bf16[64,12,512]{2,1,0:T(8,128)(2,1)S(1)} all-to-all(bf16[64,12,512]{2,1,0:T(8,128)(2,1)S(1)} %get-tuple-element.9), channel_id=1, replica_groups=mesh['seq'=64,'tp'=4] {'seq'}, dimensions={0} | all-to-all | bytes 1572864 | tf_op jit(solution)/shard_map/all_to_all | solution.py:145
  210.6 1.1 reshape.247
  211.8 1.2 all-gather.6.cloned.1.call-done
  213.0 2.7 fusion.3
  215.8 3.8 fusion.27
  219.6 7.6 %convolution_convert_fusion.1 = bf16[768,2048]{1,0:T(8,128)(2,1)} fusion(bf16[1,352,2048]{2,1,0:T(8,128)(2,1)} %param.25, bf16[1,2048,352]{1,2,0:T(8,128)(2,1)} %param.24, f32[768,352]{0,1:T(8,128)} %fusion.27, bf16[768,2048]{1,0:T(8,128)(2,1)S(1)} %copy-done.4, f32[2048]{0:T(1024)S(1)} %copy-done.12, f32[768]{0:T(1024)S(1)} %add_rsqrt_fusion.1), kind=kOutput, calls=%fused_computation.27 | convolution fusion | flops 2224078848 | bytes 10267648 | tf_op jit(solution)/shard_map/dot_general | solution.py:157
  227.2 0.3 reduce-scatter.5.cloned.1.call-start
  227.5 29.6 %all-gather.8.cloned.1.call-done = bf16[768,2048]{1,0:T(8,128)(2,1)} async-done(((bf16[768,512]{1,0:T(8,128)(2,1)}), bf16[768,2048]{1,0:T(8,128)(2,1)}) %all-gather.8.cloned.1.call-update) | async-done | bytes 3145744 | tf_op jit(solution)/shard_map/all_gather | solution.py:148
  257.1 2.7 fusion.6
  259.9 3.8 fusion.25
  263.7 7.6 %convolution_convert_fusion = bf16[768,2048]{1,0:T(8,128)(2,1)} fusion(bf16[1,352,2048]{2,1,0:T(8,128)(2,1)} %param.25, bf16[1,2048,352]{1,2,0:T(8,128)(2,1)} %param.24, f32[768,352]{0,1:T(8,128)} %fusion.25, bf16[768,2048]{1,0:T(8,128)(2,1)S(1)} %copy-done.3, f32[768]{0:T(1024)S(1)} %add_rsqrt_fusion, f32[2048]{0:T(1024)S(1)} %copy-done.12), kind=kOutput, calls=%fused_computation.26 | convolution fusion | flops 2224078848 | bytes 10267648 | tf_op jit(solution)/shard_map/dot_general | solution.py:157
  271.3 29.3 %reduce-scatter.3.cloned.1.call-done = bf16[768,512]{1,0:T(8,128)(2,1)} async-done(((bf16[768,2048]{1,0:T(8,128)(2,1)}), bf16[768,512]{1,0:T(8,128)(2,1)}) %reduce-scatter.3.cloned.1.call-update) | async-done | bytes 786448 | tf_op jit(solution)/shard_map/reduce_scatter | solution.py:160
  300.6 2.1 reshape.246
  302.8 10.9 %all-to-all-start.2 = ((bf16[64,12,512]{2,1,0:T(8,128)(2,1)}), bf16[64,12,512]{2,1,0:T(8,128)(2,1)S(1)}, u32[]{:S(2)}, u32[]{:S(2)}) async-start(bf16[64,12,512]{2,1,0:T(8,128)(2,1)} %reshape.246), calls=%async_computation.3 | async-start | bytes 2097152 | tf_op jit(solution)/shard_map/all_to_all | solution.py:163
  313.6 30.0 %reduce-scatter.5.cloned.1.call-done = bf16[768,512]{1,0:T(8,128)(2,1)} async-done(((bf16[768,2048]{1,0:T(8,128)(2,1)}), bf16[768,512]{1,0:T(8,128)(2,1)}) %reduce-scatter.5.cloned.1.call-update) | async-done | bytes 786448 | tf_op jit(solution)/shard_map/reduce_scatter | solution.py:160
  343.7 2.2 reshape.248
  345.8 10.9 %all-to-all-start.4 = ((bf16[64,12,512]{2,1,0:T(8,128)(2,1)}), bf16[64,12,512]{2,1,0:T(8,128)(2,1)}, u32[]{:S(2)}, u32[]{:S(2)}) async-start(bf16[64,12,512]{2,1,0:T(8,128)(2,1)} %reshape.248), calls=%async_computation.6 | async-start | bytes 2097152 | tf_op jit(solution)/shard_map/all_to_all | solution.py:163
  356.8 0.1 mul.276
  357.0 28.2 %all-to-all-done.4 = bf16[64,12,512]{2,1,0:T(8,128)(2,1)} async-done(((bf16[64,12,512]{2,1,0:T(8,128)(2,1)}), bf16[64,12,512]{2,1,0:T(8,128)(2,1)}, u32[]{:S(2)}, u32[]{:S(2)}) %all-to-all-start.4) | async-done | bytes 786464 | tf_op jit(solution)/shard_map/all_to_all | solution.py:163
  385.2 1.7 pad_maximum_fusion
  386.9 2.7 gather_fusion
  389.6 0.3 reshape.250
  389.9 1.1 fusion.93
  391.0 1.1 fusion.67
  392.2 11.7 %all_to_all.32 = bf16[4,128,512]{2,1,0:T(8,128)(2,1)S(1)} all-to-all(bf16[4,128,512]{2,1,0:T(8,128)(2,1)S(1)} %broadcast_in_dim.20), channel_id=1, replica_groups=mesh['seq'=64,'tp'=4] {'tp'}, dimensions={0} | all-to-all | bytes 1048576 | tf_op jit(solution)/shard_map/all_to_all | solution.py:176
  403.9 0.3 copy.111
  404.2 1.0 copy.112
  (58 shorter events, 1.2 us)
Async XLA Ops:
  7.2 1.9 copy-start
  7.2 5.2 %copy-start.2 = (bf16[128,2048]{1,0:T(8,128)(2,1)S(1)}, bf16[128,2048]{1,0:T(8,128)(2,1)}, u32[]{:S(2)}) copy-start(bf16[128,2048]{1,0:T(8,128)(2,1)} %param.13) | copy-start | bytes 1572868
  7.2 4.0 copy-start.11
  7.2 4.8 %copy-start.9 = (s32[128,6]{0,1:T(8,128)S(1)}, s32[128,6]{0,1:T(8,128)}, u32[]{:S(2)}) copy-start(s32[128,6]{0,1:T(8,128)} %param.21) | copy-start | bytes 9220
  7.2 96.3 %all-gather.4.cloned.1.call-start = ((), (), s32[]{:S(2)}) async-start(), calls=%async_computation.8 | async-start | bytes 9584640 | tf_op jit(solution)/shard_map/all_gather | solution.py:84
  9.0 6.1 %copy-start.8 = (bf16[2,512,256]{2,1,0:T(8,128)(2,1)S(1)}, bf16[2,512,256]{2,1,0:T(8,128)(2,1)}, u32[]{:S(2)}) copy-start(bf16[2,512,256]{2,1,0:T(8,128)(2,1)} %param.18) | copy-start | bytes 1572868
  113.1 7.2 %copy-start.7 = (bf16[256,2048]{1,0:T(8,128)(2,1)S(1)}, bf16[256,2048]{1,0:T(8,128)(2,1)}, u32[]{:S(2)}) copy-start(bf16[256,2048]{1,0:T(8,128)(2,1)} %param.19) | copy-start | bytes 3145732
  121.5 13.0 %all-to-all-start = ((bf16[4,128,512]{2,1,0:T(8,128)(2,1)}), bf16[4,128,512]{2,1,0:T(8,128)(2,1)S(1)}, u32[]{:S(2)}, u32[]{:S(2)}) async-start(bf16[4,128,512]{2,1,0:T(8,128)(2,1)} %bitcast.120), calls=%async_computation | async-start | bytes 1048576 | tf_op jit(solution)/shard_map/all_to_all | solution.py:116
  125.4 87.6 %all-gather.6.cloned.1.call-start = ((), (), s32[]{:S(2)}) async-start(), calls=%async_computation.9 | async-start | bytes 3932160 | tf_op jit(solution)/shard_map/all_gather | solution.py:148
  134.5 0.7 copy-start.5
  176.0 81.1 %all-gather.8.cloned.1.call-start = ((), (), s32[]{:S(2)}) async-start(), calls=%async_computation.11 | async-start | bytes 3932160 | tf_op jit(solution)/shard_map/all_gather | solution.py:148
  210.6 5.2 %copy-start.12 = (f32[2048]{0:T(1024)S(1)}, f32[2048]{0:T(1024)}, u32[]{:S(2)}) copy-start(f32[2048]{0:T(1024)} %param.20) | copy-start | bytes 24580
  211.7 88.9 %reduce-scatter.3.cloned.1.call-start = ((), (), s32[]{:S(2)}) async-start(), calls=%async_computation.10 | async-start | bytes 3932160 | tf_op jit(solution)/shard_map/reduce_scatter | solution.py:160
  213.0 2.8 copy-start.4
  227.2 116.4 %reduce-scatter.5.cloned.1.call-start = ((), (), s32[]{:S(2)}) async-start(), calls=%async_computation.12 | async-start | bytes 3932160 | tf_op jit(solution)/shard_map/reduce_scatter | solution.py:160
  257.1 2.8 copy-start.3
  302.8 54.2 %copy-start.10 = (f32[128,6]{0,1:T(8,128)S(1)}, f32[128,6]{0,1:T(8,128)}, u32[]{:S(2)}) copy-start(f32[128,6]{0,1:T(8,128)} %param.22) | copy-start | bytes 9220
  302.8 43.1 %all-to-all-start.2 = ((bf16[64,12,512]{2,1,0:T(8,128)(2,1)}), bf16[64,12,512]{2,1,0:T(8,128)(2,1)S(1)}, u32[]{:S(2)}, u32[]{:S(2)}) async-start(bf16[64,12,512]{2,1,0:T(8,128)(2,1)} %reshape.246), calls=%async_computation.3 | async-start | bytes 2097152 | tf_op jit(solution)/shard_map/all_to_all | solution.py:163
  345.8 39.4 %all-to-all-start.4 = ((bf16[64,12,512]{2,1,0:T(8,128)(2,1)}), bf16[64,12,512]{2,1,0:T(8,128)(2,1)}, u32[]{:S(2)}, u32[]{:S(2)}) async-start(bf16[64,12,512]{2,1,0:T(8,128)(2,1)} %reshape.248), calls=%async_computation.6 | async-start | bytes 2097152 | tf_op jit(solution)/shard_map/all_to_all | solution.py:163
  389.9 1.2 copy-start.6
  389.9 15.3 %copy-start.1 = (bf16[2048,576]{0,1:T(8,128)(2,1)S(1)}, bf16[2048,576]{0,1:T(8,128)(2,1)}, u32[]{:S(2)}) copy-start(bf16[2048,576]{0,1:T(8,128)(2,1)} %param.16) | copy-start | bytes 7077892
Sparse Core Ops, SparseCore 0:
  12.1 91.3 all-gather.3
  176.1 36.8 all-gather.5
  214.8 42.2 all-gather.7
  259.5 41.1 reduce-scatter.2
  303.0 40.5 reduce-scatter.4
where the time goes:
time: 412 us
  waiting for transfers between devices  211 us (51%)
  blocking collectives  85.4 us (21%)
  matrix products  41.3 us (10%)
  starting transfers between devices  26.2 us (6%)
  other arithmetic  18 us (4%)
  local copies, waits for them, and re-layouts  15.3 us (4%)
  between operations  14.2 us (3%)
    all_gather x1, waiting for transfers between devices, on_device(): shard_rows = lax.all_gather(latent, 'seq', axis=0, tiled=True)  84.7 us
    all_to_all x2, blocking collectives, on_device(): lax.all_to_all(sending, 'seq', split_axis=0, concat_axis=0, tiled=True)  73.7 us
    reduce_scatter x2, waiting for transfers between devices, on_device(): lax.psum_scatter(expert_out, 'tp', scatter_dimension=1, tiled=True)  59.3 us
    all_gather x2, waiting for transfers between devices, on_device(): lax.all_gather(flat_part, 'tp', axis=1, tiled=True).astype(jnp.float32)  30.8 us
    all_to_all x2, waiting for transfers between devices, on_device(): lax.all_to_all(expert_sum, 'seq', split_axis=0, concat_axis=0, tiled=True)  28.2 us
    all_to_all x2, starting transfers between devices, on_device(): lax.all_to_all(expert_sum, 'seq', split_axis=0, concat_axis=0, tiled=True)  21.8 us
    dot_general x2, matrix products, on_device(): jnp.dot(hidden_units, expert_down[0], preferred_element_type=jnp.float32)  15.2 us
    all_to_all x1, blocking collectives, on_device(): lax.all_to_all(repeated_part, 'tp', split_axis=0, concat_axis=0, tiled=True)  11.7 us
  transfers between devices with their start and end apart: 8, of which 7 were waited for; matrix products, arithmetic and copies ran while one was open for 10% of the time, Pallas kernels for 0%

commit v1 on v0

--- a/solution.py
+++ b/solution.py
@@ -81,7 +81,11 @@
     row_segment = jnp.repeat(segment, head_count)
     row_index = jnp.repeat(token_index, head_count)
     row_total = tok_count * head_count
-    shard_rows = lax.all_gather(latent, "seq", axis=0, tiled=True)
+    devices = lax.axis_size("seq")
+    repeats = [devices if d == 0 else 1 for d in range(latent.ndim)]
+    shard_rows = lax.all_to_all(
+        jnp.tile(latent, repeats), "seq", split_axis=0, concat_axis=0, tiled=True
+    )
     key_count = shard_rows.shape[0]
     key_index = jnp.arange(key_count, dtype=jnp.int32)
     key_segment, unused = place(key_index, lengths)

time: 412 us -> 558 us (1.35)
  waiting for transfers between devices: 211 us -> 330 us
  local copies, waits for them, and re-layouts: 15.3 us -> 33.1 us
  starting transfers between devices: 26.2 us -> 39.7 us
    all_to_all x0 -> x1, waiting for transfers between devices: none -> 203 us  [on_device(): lax.all_to_all(jnp.tile(latent, repeats), 'seq', split_axis=0, concat_axi...]
    all_gather x1 -> x0, waiting for transfers between devices: 84.7 us -> none  [on_device(): shard_rows = lax.all_gather(latent, 'seq', axis=0, tiled=True)]
    all_to_all x0 -> x1, starting transfers between devices: none -> 13.5 us  [on_device(): lax.all_to_all(jnp.tile(latent, repeats), 'seq', split_axis=0, concat_axi...]
    all_to_all x0 -> x1, local copies, waits for them, and re-layouts: none -> 8.73 us  [on_device(): lax.all_to_all(jnp.tile(latent, repeats), 'seq', split_axis=0, concat_axi...]
    another operation x0 -> x1, local copies, waits for them, and re-layouts: none -> 5.93 us  [on_device(): jnp.tile(latent, repeats)]
  transfers between devices with their start and end apart: 8 -> 8, of which waited for: 7 -> 7; matrix products, arithmetic and copies ran while one was open for 10% -> 7% of each run, Pallas kernels for 0% -> 0%
where the time goes in v1:
time: 558 us; the launch traced here: 557 us
  waiting for transfers between devices  330 us (59%)
  blocking collectives  80.1 us (14%)
  matrix products  42 us (8%)
  starting transfers between devices  39.7 us (7%)
  local copies, waits for them, and re-layouts  33.1 us (6%)
  other arithmetic  17.3 us (3%)
  between operations  14.3 us (3%)
    all_to_all x1, waiting for transfers between devices, on_device(): lax.all_to_all(jnp.tile(latent, repeats), 'seq', split_axis=0, concat_axi...  203 us
    all_to_all x2, blocking collectives, on_device(): lax.all_to_all(sending, 'seq', split_axis=0, concat_axis=0, tiled=True)  68.4 us
    reduce_scatter x2, waiting for transfers between devices, on_device(): lax.psum_scatter(expert_out, 'tp', scatter_dimension=1, tiled=True)  59.9 us
    all_gather x2, waiting for transfers between devices, on_device(): lax.all_gather(flat_part, 'tp', axis=1, tiled=True).astype(jnp.float32)  30.2 us
    all_to_all x2, waiting for transfers between devices, on_device(): lax.all_to_all(expert_sum, 'seq', split_axis=0, concat_axis=0, tiled=True)  28.2 us
    all_to_all x2, starting transfers between devices, on_device(): lax.all_to_all(expert_sum, 'seq', split_axis=0, concat_axis=0, tiled=True)  21.8 us
    dot_general x2, matrix products, on_device(): jnp.dot(hidden_units, expert_down[0], preferred_element_type=jnp.float32)  16.7 us
    all_to_all x1, starting transfers between devices, on_device(): lax.all_to_all(jnp.tile(latent, repeats), 'seq', split_axis=0, concat_axi...  13.5 us
  transfers between devices with their start and end apart: 8, of which 7 were waited for; matrix products, arithmetic and copies ran while one was open for 7% of the time, Pallas kernels for 0%

profile of v1, /device:TPU:1, one launch (start us, length us, event | category | flops | bytes accessed | tf_op | source)
XLA Modules:
  0.0 556.8 jit_solution(14363406447608806796)
XLA Ops:
  7.2 1.0 reduce-window.18
  8.2 0.7 fusion.82
  9.0 1.8 fusion.94
  10.9 0.1 multiply_cosine_fusion
  11.1 0.1 multiply_convert_fusion
  11.2 5.9 %tile.2 = bf16[64,128,576]{1,2,0:T(8,128)(2,1)} broadcast(bf16[128,576]{0,1:T(8,128)(2,1)S(1)} %pad_maximum_fusion.1), dimensions={1,2} | broadcast | bytes 9584640 | tf_op jit(solution)/shard_map/tile | solution.py:87
  17.2 13.5 %all-to-all-start = ((bf16[64,128,576]{1,2,0:T(8,128)(2,1)}), bf16[64,128,576]{1,2,0:T(8,128)(2,1)}, u32[]{:S(2)}, u32[]{:S(2)}) async-start(bf16[64,128,576]{1,2,0:T(8,128)(2,1)} %tile.2), calls=%async_computation | async-start | bytes 18874368 | tf_op jit(solution)/shard_map/all_to_all | solution.py:86
  30.8 0.1 eq.62
  30.9 0.1 eq.58
  31.1 0.4 convolution_convert_fusion.4
  32.0 0.2 eq.54
  32.2 0.2 le.48
  32.4 0.3 convolution_bitcast_fusion
  32.6 0.4 copy.99
  33.1 0.4 concatenate.21
  33.5 1.8 reduce-window.19
  35.3 0.3 slice_reduce_fusion
  35.6 0.1 fusion.76
  35.7 0.1 reduce_sum.104
  35.8 0.2 convert_reduce_fusion.1
  36.0 202.9 %all-to-all-done = bf16[64,128,576]{1,2,0:T(8,128)(2,1)} async-done(((bf16[64,128,576]{1,2,0:T(8,128)(2,1)}), bf16[64,128,576]{1,2,0:T(8,128)(2,1)}, u32[]{:S(2)}, u32[]{:S(2)}) %all-to-all-start) | async-done | bytes 9437216 | tf_op jit(solution)/shard_map/all_to_all | solution.py:86
  238.9 6.7 %select_reduce_fusion = (f32[256]{0:T(256)S(1)}, f32[256,8192]{1,0:T(8,128)S(1)}) fusion(s32[256]{0:T(256)S(1)} %le.48, s32[8192]{0:T(1024)S(1)} %convert_reduce_fusion.1, s32[256]{0:T(256)S(1)} %eq.54, f32[256,32]{1,0:T(8,128)S(1)} %bitcast.140, f32[256,32]{1,0:T(8,128)S(1)} %bitcast.139, f32[256,512]{1,0:T(8,128)S(1)} %concatenate.21, ...), kind=kOutput, calls=%fused_computation.5 | convolution fusion | flops 2426994432 | bytes 18451456 | tf_op jit(solution)/shard_map/ra,ka->rk/dot_general | solution.py:96
  245.6 3.3 copy-done.2
  248.9 2.7 fusion.9
  251.7 8.7 %copy_bitcast_fusion = bf16[8192,576]{0,1:T(8,128)(2,1)} fusion(bf16[64,128,576]{1,2,0:T(8,128)(2,1)} %all-to-all-done), kind=kLoop, calls=%fused_computation.1 | loop fusion | bytes 18874368 | tf_op jit(solution)/shard_map/all_to_all | solution.py:86
  260.4 8.4 %fusion.41 = f32[256,512]{1,0:T(8,128)S(1)} fusion(bf16[8192,576]{0,1:T(8,128)(2,1)} %copy_bitcast_fusion, f32[256,8192]{1,0:T(8,128)} %copy-done.2, f32[256]{0:T(256)S(1)} %broadcast_maximum_fusion, s32[256]{0:T(256)S(1)} %le.48, s32[8192]{0:T(1024)S(1)} %convert_reduce_fusion.1, s32[256]{0:T(256)S(1)} %eq.54, f32[256]{0:T(256)S(1)} %fusion.9), kind=kOutput, calls=%fused_computation.50 | convolution fusion | flops 2160197632 | bytes 17338368 | tf_op jit(solution)/shard_map/dot_general | solution.py:101
  268.8 0.3 reshape.268
  269.1 0.5 convolution_convert_fusion.5
  269.6 0.3 convolution_convert_fusion.3
  269.9 0.8 copy.153
  270.8 4.0 all-to-all-start.1
  274.9 0.7 fusion.18
  275.6 9.1 %all-to-all-done.1 = bf16[4,128,512]{2,1,0:T(8,128)(2,1)S(1)} async-done(((bf16[4,128,512]{2,1,0:T(8,128)(2,1)}), bf16[4,128,512]{2,1,0:T(8,128)(2,1)S(1)}, u32[]{:S(2)}, u32[]{:S(2)}) %all-to-all-start.1) | async-done | bytes 524320 | tf_op jit(solution)/shard_map/all_to_all | solution.py:120
  284.8 0.6 convolution_convert_fusion.2
  285.4 0.5 fusion.92
  285.8 33.9 %all_to_all.39 = bf16[64,12,512]{2,1,0:T(8,128)(2,1)S(1)} all-to-all(bf16[64,12,512]{2,1,0:T(8,128)(2,1)S(1)} %get-tuple-element.8), channel_id=1, replica_groups=mesh['seq'=64,'tp'=4] {'seq'}, dimensions={0} | all-to-all | bytes 1572864 | tf_op jit(solution)/shard_map/all_to_all | solution.py:149
  319.8 1.1 reshape.273
  320.9 34.5 %all_to_all.40 = bf16[64,12,512]{2,1,0:T(8,128)(2,1)S(1)} all-to-all(bf16[64,12,512]{2,1,0:T(8,128)(2,1)S(1)} %get-tuple-element.9), channel_id=1, replica_groups=mesh['seq'=64,'tp'=4] {'seq'}, dimensions={0} | all-to-all | bytes 1572864 | tf_op jit(solution)/shard_map/all_to_all | solution.py:149
  355.4 1.0 reshape.275
  356.5 1.3 all-gather.3.cloned.1.call-done
  357.8 2.7 fusion.3
  360.7 3.9 fusion.27
  364.6 8.1 %convolution_convert_fusion.1 = bf16[768,2048]{1,0:T(8,128)(2,1)} fusion(bf16[1,352,2048]{2,1,0:T(8,128)(2,1)S(1)} %copy-done.16, bf16[1,2048,352]{1,2,0:T(8,128)(2,1)} %param.24, f32[768,352]{0,1:T(8,128)} %fusion.27, bf16[768,2048]{1,0:T(8,128)(2,1)} %all-gather.3.cloned.1.call-done, f32[2048]{0:T(1024)S(1)} %copy-done.17, f32[768]{0:T(1024)S(1)} %add_rsqrt_fusion.1), kind=kOutput, calls=%fused_computation.28 | convolution fusion | flops 2224078848 | bytes 10267648 | tf_op jit(solution)/shard_map/dot_general | solution.py:161
  372.7 0.3 reduce-scatter.5.cloned.1.call-start
  373.0 28.9 %all-gather.5.cloned.1.call-done = bf16[768,2048]{1,0:T(8,128)(2,1)} async-done(((bf16[768,512]{1,0:T(8,128)(2,1)}), bf16[768,2048]{1,0:T(8,128)(2,1)}) %all-gather.5.cloned.1.call-update) | async-done | bytes 3145744 | tf_op jit(solution)/shard_map/all_gather | solution.py:152
  401.9 2.7 fusion.6
  404.7 2.4 fusion.25
  407.1 8.6 %convolution_convert_fusion = bf16[768,2048]{1,0:T(8,128)(2,1)} fusion(bf16[1,352,2048]{2,1,0:T(8,128)(2,1)} %param.25, bf16[1,2048,352]{1,2,0:T(8,128)(2,1)} %param.24, f32[768,352]{0,1:T(8,128)} %fusion.25, bf16[768,2048]{1,0:T(8,128)(2,1)} %all-gather.5.cloned.1.call-done, f32[768]{0:T(1024)S(1)} %add_rsqrt_fusion, f32[2048]{0:T(1024)S(1)} %copy-done.17), kind=kOutput, calls=%fused_computation.27 | convolution fusion | flops 2224078848 | bytes 10267648 | tf_op jit(solution)/shard_map/dot_general | solution.py:161
  415.7 29.9 %reduce-scatter.3.cloned.1.call-done = bf16[768,512]{1,0:T(8,128)(2,1)} async-done(((bf16[768,2048]{1,0:T(8,128)(2,1)}), bf16[768,512]{1,0:T(8,128)(2,1)}) %reduce-scatter.3.cloned.1.call-update) | async-done | bytes 786448 | tf_op jit(solution)/shard_map/reduce_scatter | solution.py:164
  445.6 2.1 reshape.274
  447.8 10.9 %all-to-all-start.3 = ((bf16[64,12,512]{2,1,0:T(8,128)(2,1)}), bf16[64,12,512]{2,1,0:T(8,128)(2,1)S(1)}, u32[]{:S(2)}, u32[]{:S(2)}) async-start(bf16[64,12,512]{2,1,0:T(8,128)(2,1)} %reshape.274), calls=%async_computation.4 | async-start | bytes 2097152 | tf_op jit(solution)/shard_map/all_to_all | solution.py:167
  458.6 30.0 %reduce-scatter.5.cloned.1.call-done = bf16[768,512]{1,0:T(8,128)(2,1)} async-done(((bf16[768,2048]{1,0:T(8,128)(2,1)}), bf16[768,512]{1,0:T(8,128)(2,1)}) %reduce-scatter.5.cloned.1.call-update) | async-done | bytes 786448 | tf_op jit(solution)/shard_map/reduce_scatter | solution.py:164
  488.7 2.2 reshape.276
  490.8 10.9 %all-to-all-start.5 = ((bf16[64,12,512]{2,1,0:T(8,128)(2,1)}), bf16[64,12,512]{2,1,0:T(8,128)(2,1)}, u32[]{:S(2)}, u32[]{:S(2)}) async-start(bf16[64,12,512]{2,1,0:T(8,128)(2,1)} %reshape.276), calls=%async_computation.7 | async-start | bytes 2097152 | tf_op jit(solution)/shard_map/all_to_all | solution.py:167
  501.8 0.1 mul.276
  502.0 28.2 %all-to-all-done.5 = bf16[64,12,512]{2,1,0:T(8,128)(2,1)} async-done(((bf16[64,12,512]{2,1,0:T(8,128)(2,1)}), bf16[64,12,512]{2,1,0:T(8,128)(2,1)}, u32[]{:S(2)}, u32[]{:S(2)}) %all-to-all-start.5) | async-done | bytes 786464 | tf_op jit(solution)/shard_map/all_to_all | solution.py:167
  530.2 1.7 pad_maximum_fusion
  531.9 2.7 gather_fusion
  534.6 0.3 reshape.278
  534.9 1.1 fusion.93
  536.0 1.1 fusion.67
  537.2 11.7 %all_to_all.41 = bf16[4,128,512]{2,1,0:T(8,128)(2,1)S(1)} all-to-all(bf16[4,128,512]{2,1,0:T(8,128)(2,1)S(1)} %broadcast_in_dim.20), channel_id=1, replica_groups=mesh['seq'=64,'tp'=4] {'tp'}, dimensions={0} | all-to-all | bytes 1048576 | tf_op jit(solution)/shard_map/all_to_all | solution.py:180
  548.9 0.3 copy.116
  549.2 1.0 copy.117
  (69 shorter events, 1.4 us)
Async XLA Ops:
  7.2 1.8 copy-start
  7.2 3.9 copy-start.14
  11.2 5.9 %copy-start.10 = (bf16[128,576]{0,1:T(8,128)(2,1)}, bf16[128,576]{0,1:T(8,128)(2,1)S(1)}, u32[]{:S(2)}) copy-start(bf16[128,576]{0,1:T(8,128)(2,1)S(1)} %pad_maximum_fusion.1) | copy-start | bytes 442372
  17.2 13.5 %copy-start.12 = (s32[128,6]{0,1:T(8,128)S(1)}, s32[128,6]{0,1:T(8,128)}, u32[]{:S(2)}) copy-start(s32[128,6]{0,1:T(8,128)} %param.21) | copy-start | bytes 9220
  17.2 13.9 %copy-start.3 = (bf16[128,2048]{1,0:T(8,128)(2,1)S(1)}, bf16[128,2048]{1,0:T(8,128)(2,1)}, u32[]{:S(2)}) copy-start(bf16[128,2048]{1,0:T(8,128)(2,1)} %param.13) | copy-start | bytes 1572868
  17.2 13.9 %copy-start.8 = (bf16[2048,384]{1,0:T(8,128)(2,1)S(1)}, bf16[2048,384]{1,0:T(8,128)(2,1)}, u32[]{:S(2)}) copy-start(bf16[2048,384]{1,0:T(8,128)(2,1)} %param.15) | copy-start | bytes 4718596
  17.2 221.7 %all-to-all-start = ((bf16[64,128,576]{1,2,0:T(8,128)(2,1)}), bf16[64,128,576]{1,2,0:T(8,128)(2,1)}, u32[]{:S(2)}, u32[]{:S(2)}) async-start(bf16[64,128,576]{1,2,0:T(8,128)(2,1)} %tile.2), calls=%async_computation | async-start | bytes 18874368 | tf_op jit(solution)/shard_map/all_to_all | solution.py:86
  30.6 1.7 copy-start.11
  245.6 3.4 copy-start.2
  260.4 9.2 %copy-start.9 = (bf16[256,2048]{1,0:T(8,128)(2,1)S(1)}, bf16[256,2048]{1,0:T(8,128)(2,1)}, u32[]{:S(2)}) copy-start(bf16[256,2048]{1,0:T(8,128)(2,1)} %param.19) | copy-start | bytes 3145732
  270.8 13.9 %all-to-all-start.1 = ((bf16[4,128,512]{2,1,0:T(8,128)(2,1)}), bf16[4,128,512]{2,1,0:T(8,128)(2,1)S(1)}, u32[]{:S(2)}, u32[]{:S(2)}) async-start(bf16[4,128,512]{2,1,0:T(8,128)(2,1)} %bitcast.130), calls=%async_computation.1 | async-start | bytes 1048576 | tf_op jit(solution)/shard_map/all_to_all | solution.py:120
  274.8 83.0 %all-gather.3.cloned.1.call-start = ((), (), s32[]{:S(2)}) async-start(), calls=%async_computation.9 | async-start | bytes 3932160 | tf_op jit(solution)/shard_map/all_gather | solution.py:152
  284.8 1.1 copy-start.6
  320.8 81.1 %all-gather.5.cloned.1.call-start = ((), (), s32[]{:S(2)}) async-start(), calls=%async_computation.11 | async-start | bytes 3932160 | tf_op jit(solution)/shard_map/all_gather | solution.py:152
  355.4 5.2 copy-start.17
  356.5 89.2 %reduce-scatter.3.cloned.1.call-start = ((), (), s32[]{:S(2)}) async-start(), calls=%async_computation.10 | async-start | bytes 3932160 | tf_op jit(solution)/shard_map/reduce_scatter | solution.py:164
  357.8 2.8 copy-start.5
  360.7 3.9 copy-start.16
  372.7 32.0 %copy-start.15 = (bf16[1,2048,352]{1,2,0:T(8,128)(2,1)S(1)}, bf16[1,2048,352]{1,2,0:T(8,128)(2,1)}, u32[]{:S(2)}) copy-start(bf16[1,2048,352]{1,2,0:T(8,128)(2,1)} %param.23) | copy-start | bytes 4325380
  372.7 115.9 %reduce-scatter.5.cloned.1.call-start = ((), (), s32[]{:S(2)}) async-start(), calls=%async_computation.12 | async-start | bytes 3932160 | tf_op jit(solution)/shard_map/reduce_scatter | solution.py:164
  401.9 2.8 copy-start.4
  447.8 54.2 %copy-start.13 = (f32[128,6]{0,1:T(8,128)S(1)}, f32[128,6]{0,1:T(8,128)}, u32[]{:S(2)}) copy-start(f32[128,6]{0,1:T(8,128)} %param.22) | copy-start | bytes 9220
  447.8 43.1 %all-to-all-start.3 = ((bf16[64,12,512]{2,1,0:T(8,128)(2,1)}), bf16[64,12,512]{2,1,0:T(8,128)(2,1)S(1)}, u32[]{:S(2)}, u32[]{:S(2)}) async-start(bf16[64,12,512]{2,1,0:T(8,128)(2,1)} %reshape.274), calls=%async_computation.4 | async-start | bytes 2097152 | tf_op jit(solution)/shard_map/all_to_all | solution.py:167
  490.8 39.4 %all-to-all-start.5 = ((bf16[64,12,512]{2,1,0:T(8,128)(2,1)}), bf16[64,12,512]{2,1,0:T(8,128)(2,1)}, u32[]{:S(2)}, u32[]{:S(2)}) async-start(bf16[64,12,512]{2,1,0:T(8,128)(2,1)} %reshape.276), calls=%async_computation.7 | async-start | bytes 2097152 | tf_op jit(solution)/shard_map/all_to_all | solution.py:167
  534.9 1.2 copy-start.7
  534.9 15.3 %copy-start.1 = (bf16[2048,576]{0,1:T(8,128)(2,1)S(1)}, bf16[2048,576]{0,1:T(8,128)(2,1)}, u32[]{:S(2)}) copy-start(bf16[2048,576]{0,1:T(8,128)(2,1)} %param.16) | copy-start | bytes 7077892
Sparse Core Ops, SparseCore 0:
  321.0 36.8 all-gather.2
  359.6 42.2 all-gather.4
  404.5 41.1 reduce-scatter.2
  448.0 40.5 reduce-scatter.4
